TPU v7x, 128 devices: a whole 4x4x4 slice. The times are simulated.
128 devices in a mesh: seq: 2 (over y_lo), col: 16 (over y_hi, z, core), tp: 4 (over x).
Axes of the slice: x: 4, y: 4 (y_hi: 2, y_lo: 2; y = y_hi * 2 + y_lo), z: 4, core: 2. Of those that a mesh axis runs over, the one named last changes fastest.
Arguments:
- inputs: bfloat16 [4096, 8192], P(('seq', 'tp'), 'col'), may hold values from -6 to 6
- grads: bfloat16 [4096, 8192], P(('seq', 'tp'), 'col'), may hold values from -0.035888672 to 0.035888672
- h_in: bfloat16 [8192, 8192], P(None, 'col'), may hold values from -0.0625 to 0.0625
- segments: int32 [8, 512], P(('seq', 'tp')), may hold values from 0 to 3, never falling along the last dimension, each value on 1 to 256 neighbouring positions
Outputs:
- h_out: float32 [8192, 8192], P(('seq', 'tp'), 'col')
Inputs may be any that keep to these rules, and one draw needn't show every extreme that they name: `segments`: within each sequence the numbers never fall; every document has 1 to 256 tokens.
All inputs are finite; a program needn't handle non-finite values.
Results may differ from a plain program's by a relative error of at most 0.005.
Values may be sent and summed in bfloat16 or wider, within the bound.
No kernel may reach another device: no remote copies, remote signals or barrier semaphores. Data moves between devices by JAX's collectives and lax.ppermute only.
A program may use at most 128 MiB of HBM per device.

v0:
```python
import jax
import jax.numpy as jnp
from jax import lax
from jax.sharding import PartitionSpec as P


def per_device(inputs, grads, h_in, segments):
    x_full = lax.all_gather(inputs, "col", axis=1, tiled=True)
    projected = jnp.dot(x_full, h_in, preferred_element_type=jnp.float32).astype(jnp.bfloat16)
    partials = [
        lax.dot_general(
            projected, inputs, (((1,), (1,)), ((), ())), preferred_element_type=jnp.float32
        )
    ]
    partial_squares = jnp.stack(partials)
    whole_sum = lax.psum(partial_squares, "col")
    same = segments[:, :, None] == segments[:, None, :]
    squares = jnp.where(same, whole_sum, jnp.float32(0.0)).astype(jnp.bfloat16)
    d_full = lax.all_gather(grads, "col", axis=1, tiled=True)
    sequence = 0
    products = [
        jnp.dot(squares[sequence], grads, preferred_element_type=jnp.float32).astype(jnp.bfloat16)
    ]
    sequence = 0
    accumulated = lax.dot_general(
        d_full, products[sequence], (((0,), (0,)), ((), ())), preferred_element_type=jnp.float32
    )
    return lax.psum_scatter(accumulated, ("seq", "tp"), scatter_dimension=0, tiled=True)


def solution(mesh):
    placed = (
        P(("seq", "tp"), "col"),
        P(("seq", "tp"), "col"),
        P(None, "col"),
        P(("seq", "tp"), None),
    )
    return jax.shard_map(
        per_device, mesh=mesh, in_specs=placed, out_specs=P(("seq", "tp"), "col"), check_vma=False
    )
```

profile of v0, /device:TPU:0, one launch (start us, length us, event | category | flops | bytes accessed | tf_op | source)
XLA Modules:
  0.0 376.1 jit_solution(530166121252045588)
XLA Ops:
  6.5 0.0 all-gather.3.cloned.1.call-start
  6.5 0.7 all-gather.3.cloned.1.call-update
  7.3 0.0 all-gather.5.cloned.1.call-start
  7.3 0.7 all-gather.5.cloned.1.call-update
  8.0 0.0 copy-start
  8.0 0.0 copy-start.1
  8.0 0.0 reduce-scatter.2.cloned.1.call-start
  8.1 80.6 %all-gather.3.cloned.1.call-done = bf16[512,8192]{1,0:T(8,128)(2,1)} async-done(((bf16[512,512]{1,0:T(8,128)(2,1)}), bf16[512,8192]{1,0:T(8,128)(2,1)}) %all-gather.3.cloned.1.call-update) | async-done | bytes 8388624 | tf_op jit(solution)/shard_map/all_gather | solution.py:8
  88.7 10.6 %convolution_bitcast_fusion.1 = f32[1,512,512]{2,1,0:T(8,128)S(1)} fusion(bf16[512,512]{1,0:T(8,128)(2,1)} %param.4, bf16[512,8192]{1,0:T(8,128)(2,1)} %all-gather.3.cloned.1.call-done, bf16[8192,512]{1,0:T(8,128)(2,1)} %param.6), kind=kOutput, calls=%fused_computation.1 | convolution fusion | flops 4563664896 | bytes 18350080 | tf_op jit(solution)/shard_map/dot_general | solution.py:11
  99.3 85.3 %all-reduce.1 = bf16[1,512,512]{2,1,0:T(8,128)(2,1)S(1)} all-reduce(f32[1,512,512]{2,1,0:T(8,128)S(1)} %convolution_bitcast_fusion.1), channel_id=1, replica_groups=mesh['seq'=2,'col'=16,'tp'=4] {'col'}, use_global_device_ids=true, to_apply=%region_0.0 | all-reduce | flops 262144 | bytes 1572864 | tf_op jit(solution)/shard_map/psum | solution.py:16
  184.5 0.0 all-gather.5.cloned.1.call-done
  184.6 0.0 copy-done
  184.6 0.0 copy-done.1
  184.6 12.4 %convolution_bitcast_fusion = f32[8192,512]{0,1:T(8,128)} fusion(bf16[512,8192]{1,0:T(8,128)(2,1)} %all-gather.5.cloned.1.call-done, bf16[512,512]{1,0:T(8,128)(2,1)S(1)} %copy-done, bf16[1,512,512]{2,1,0:T(8,128)(2,1)S(1)} %all-reduce.1, s32[512]{0:T(512)S(1)} %bitcast.14), kind=kOutput, calls=%fused_computation | convolution fusion | flops 4564189184 | bytes 26216448 | tf_op jit(solution)/shard_map/dot_general | solution.py:25
  197.0 0.0 reduce-scatter.2.cloned.1.call-update
  197.0 169.7 %reduce-scatter.2.cloned.1.call-done = f32[1024,512]{0,1:T(8,128)} async-done(((f32[8192,512]{0,1:T(8,128)}), f32[1024,512]{0,1:T(8,128)}) %reduce-scatter.2.cloned.1.call-update) | async-done | bytes 2097168 | tf_op jit(solution)/shard_map/reduce_scatter | solution.py:28
  366.7 2.9 copy.5
Async XLA Ops:
  6.5 82.1 %all-gather.3.cloned.1.call-start = ((), (), s32[]{:S(2)}) async-start(), calls=%async_computation.1 | async-start | bytes 8912896 | tf_op jit(solution)/shard_map/all_gather | solution.py:8
  7.3 177.3 %all-gather.5.cloned.1.call-start = ((), (), s32[]{:S(2)}) async-start(), calls=%async_computation.2 | async-start | bytes 8912896 | tf_op jit(solution)/shard_map/all_gather | solution.py:19
  8.0 176.6 %copy-start = (bf16[512,512]{1,0:T(8,128)(2,1)S(1)}, bf16[512,512]{1,0:T(8,128)(2,1)}, u32[]{:S(2)}) copy-start(bf16[512,512]{1,0:T(8,128)(2,1)} %param.5) | copy-start | bytes 1572868
  8.0 176.6 %copy-start.1 = (s32[1,512]{1,0:T(1,128)S(1)}, s32[1,512]{1,0:T(1,128)}, u32[]{:S(2)}) copy-start(s32[1,512]{1,0:T(1,128)} %param.7) | copy-start | bytes 6148
  8.0 358.7 %reduce-scatter.2.cloned.1.call-start = ((), (), s32[]{:S(2)}) async-start(), calls=%async_computation.3 | async-start | bytes 18874368 | tf_op jit(solution)/shard_map/reduce_scatter | solution.py:28
Sparse Core Ops, SparseCore 0:
  9.6 79.0 all-gather.2
  90.9 79.6 all-gather.4
  197.1 169.5 reduce-scatter.1
where the time goes:
time: 377 us; the launch traced here: 376 us
  waiting for transfers between devices  252 us (67%)
  blocking collectives  85.3 us (23%)
  matrix products  23 us (6%)
  between operations  13.2 us (4%)
    reduce_scatter x1, waiting for transfers between devices, per_device(): lax.psum_scatter(accumulated, ('seq', 'tp'), scatter_dimension=0, tiled=T...  170 us
    psum x1, blocking collectives, per_device(): whole_sum = lax.psum(partial_squares, 'col')  85.3 us
    all_gather x1, waiting for transfers between devices, per_device(): x_full = lax.all_gather(inputs, 'col', axis=1, tiled=True)  80.6 us
    dot_general x1, matrix products, per_device(): lax.dot_general(d_full, products[sequence], (((0,), (0,)), ((), ())), pre...  12.4 us
    dot_general x1, matrix products, per_device(): lax.dot_general(projected, inputs, (((1,), (1,)), ((), ())), preferred_el...  10.6 us
  transfers between devices with their start and end apart: 3, of which 2 were waited for; matrix products, arithmetic and copies ran while one was open for 3% of the time, Pallas kernels for 0%

commit v1 on v0

v1 whole, which is shorter than its diff:
```python
import jax
import jax.numpy as jnp
from jax import lax
from jax.sharding import Mesh, PartitionSpec as P

AXES = ("yl", "yh", "z", "k", "x")
SIZES = (2, 2, 4, 2, 4)
F32 = jnp.float32
BF16 = jnp.bfloat16


def linear(place):
    index = 0
    for part, size in zip(place, SIZES):
        index = index * size + part
    return index


def place_of(index):
    parts = []
    for size in reversed(SIZES):
        parts.append(index % size)
        index //= size
    return tuple(reversed(parts))


def move(value, where):
    pairs = [(i, linear(where(*place_of(i)))) for i in range(128)]
    return lax.ppermute(value, AXES, pairs)


def z_up(yl, yh, z, k, x):
    return yl, yh, (z + 1) % 4, k, x


def z_down(yl, yh, z, k, x):
    return yl, yh, (z - 1) % 4, k, x


def x_up(yl, yh, z, k, x):
    return yl, yh, z, k, (x + 1) % 4


def x_down(yl, yh, z, k, x):
    return yl, yh, z, k, (x - 1) % 4


def swap_yh(yl, yh, z, k, x):
    return yl, 1 - yh, z, k, x


def swap_yl(yl, yh, z, k, x):
    return 1 - yl, yh, z, k, x


def swap_core(yl, yh, z, k, x):
    return yl, yh, z, 1 - k, x


def z_pair_a(yl, yh, z, k, x):
    return yl, yh, z ^ 1, k, x


def z_pair_b(yl, yh, z, k, x):
    return yl, yh, (z + 1 if z % 2 else z - 1) % 4, k, x


def shear(yl, yh, z, k, x):
    return yl, yh, (z + x) % 4, k, x


def reflect(yl, yh, z, k, x):
    return yh, yl, z, k, (z - x) % 4


def gather8(own, cut, up, down, across):
    below = move(own, up)
    above = move(own, down)
    over = move(own, across)
    top = move(below[:cut], up)
    bottom = move(above[cut:], down)
    over_below = move(over, up)
    over_above = move(over, down)
    over_top = move(top, across)
    over_bottom = move(bottom, across)
    far = jnp.concatenate([top, bottom])
    over_far = jnp.concatenate([over_top, over_bottom])
    return [own, above, far, below, over, over_above, over_far, over_below]


def per_device(inputs, grads, h_in, segments):
    yl, yh, z, k, x = (lax.axis_index(name) for name in AXES)

    xs = gather8(inputs, 256, z_up, z_down, swap_yh)
    order = [(yh ^ a) * 4 + (z + b) % 4 for a in range(2) for b in range(4)]
    h_mine = jnp.concatenate(
        [lax.dynamic_slice(h_in, (i * 1024 + k * 512, 0), (512, 512)) for i in order]
    )
    h_send = jnp.concatenate(
        [lax.dynamic_slice(h_in, (i * 1024 + (1 - k) * 512, 0), (512, 512)) for i in order]
    )
    h_core = move(h_send, swap_core)
    x_half = jnp.concatenate(xs, axis=1)
    y_mine = jnp.dot(x_half, h_mine, preferred_element_type=F32)
    y_send = jnp.dot(x_half, h_core, preferred_element_type=F32)
    y = (y_mine + move(y_send, swap_core)).astype(BF16)
    p = lax.dot_general(y, inputs, (((1,), (1,)), ((), ())), preferred_element_type=F32)
    seg = segments[0]
    same = seg[:, None] == seg[None, :]
    folded = jnp.where(same[:, :256], p[:, :256], jnp.where(same[:, 256:], p[:, 256:], 0.0))
    acc = lax.dynamic_slice(folded, (k * 256, 0), (256, 256)) + move(
        lax.dynamic_slice(folded, ((1 - k) * 256, 0), (256, 256)), swap_core
    )
    for where in (swap_yh, z_pair_a, z_pair_b):
        acc = acc + move(acc.astype(BF16), where).astype(F32)
    kh = acc.astype(BF16)
    pair = jnp.stack([kh, move(kh, swap_yl)])
    below = move(pair, x_up)
    above = move(pair, x_down)
    far = jnp.stack([move(below[0], x_up), move(above[1], x_down)])
    halves = jnp.stack([pair[0], above[0], far[0], below[0], pair[1], above[1], far[1], below[1]])
    other = move(halves, swap_core)
    first = jnp.where(k == 0, halves, other)
    second = jnp.where(k == 0, other, halves)
    k_all = jnp.concatenate([first, second], axis=1)

    marked = jnp.concatenate([grads, jnp.broadcast_to(segments.astype(BF16), (16, 512))])
    ds = jnp.stack(gather8(marked, 256, x_up, x_down, swap_yl))
    d_c = ds[:, :512]
    seg_all = ds[:, 512]
    same_all = seg_all[:, :, None] == seg_all[:, None, :]
    k_full = jnp.concatenate(
        [
            jnp.where(same_all[:, :, :256], k_all, jnp.zeros((), BF16)),
            jnp.where(same_all[:, :, 256:], k_all, jnp.zeros((), BF16)),
        ],
        axis=2,
    )
    z_all = lax.dot_general(
        k_full, d_c, (((2,), (1,)), ((0,), (0,))), preferred_element_type=F32
    ).astype(BF16)

    turned = move(move(grads, shear), reflect)
    rs = gather8(turned, 256, z_up, z_down, swap_yh)
    r_mine = jnp.stack(rs)
    r_core = move(r_mine, swap_core)
    pick = jnp.stack(
        [(yl ^ a ^ yh) * 4 + (2 * x + b - z) % 4 for a in range(2) for b in range(4)]
    )
    r_mine = jnp.take(r_mine, pick, axis=0).reshape(4096, 512)
    r_core = jnp.take(r_core, pick, axis=0).reshape(4096, 512)
    z_flat = z_all.reshape(4096, 512)
    out_mine = lax.dot_general(r_mine, z_flat, (((0,), (0,)), ((), ())), preferred_element_type=F32)
    out_core = lax.dot_general(r_core, z_flat, (((0,), (0,)), ((), ())), preferred_element_type=F32)
    return jnp.concatenate(
        [jnp.where(k == 0, out_mine, out_core), jnp.where(k == 0, out_core, out_mine)]
    )


def solution(mesh):
    fine = Mesh(mesh.devices.reshape(SIZES), AXES)
    col = ("yh", "z", "k")
    row = ("yl", "x")
    return jax.shard_map(
        per_device,
        mesh=fine,
        in_specs=(P(row, col), P(row, col), P(None, col), P(row, None)),
        out_specs=P(row, col),
        check_vma=False,
    )
```

time: 377 us -> 225 us (0.60)
  waiting for transfers between devices: 252 us -> 62.9 us
  blocking collectives: 85.3 us -> 0 us
  starting transfers between devices: 0.08 us -> 79.8 us
  local copies, waits for them, and re-layouts: 2.89 us -> 47.4 us
  between operations: 13.2 us -> 0.55 us
  other arithmetic: 0 us -> 12.5 us
    reduce_scatter x1 -> x0, waiting for transfers between devices: 170 us -> none  [per_device(): lax.psum_scatter(accumulated, ('seq', 'tp'), scatter_dimension=0, tiled=T...]
    psum x1 -> x0, blocking collectives: 85.3 us -> none  [per_device(): whole_sum = lax.psum(partial_squares, 'col')]
    all_gather x2 -> x0, waiting for transfers between devices: 80.6 us -> none  [the longest x1 80.6 us: per_device(): x_full = lax.all_gather(inputs, 'col', axis=1, tiled=True)]
    ppermute x0 -> x42, starting transfers between devices: none -> 79.8 us  [move(): return lax.ppermute(value, AXES, pairs)]
    ppermute x0 -> x42, waiting for transfers between devices: none -> 62.9 us  [move(): return lax.ppermute(value, AXES, pairs)]
    unnamed x4 -> x44, local copies, waits for them, and re-layouts: 0.01 us -> 29.2 us
    gather x0 -> x2, local copies, waits for them, and re-layouts: none -> 10.1 us  [the longest x1 5.06 us: per_device(): r_core = jnp.take(r_core, pick, axis=0).reshape(4096, 512)]
    unnamed x0 -> x9, other arithmetic: none -> 6.37 us
  transfers between devices with their start and end apart: 3 -> 42, of which waited for: 2 -> 14; matrix products, arithmetic and copies ran while one was open for 3% -> 21% of each run, Pallas kernels for 0% -> 0%
where the time goes in v1:
time: 225 us; the launch traced here: 224 us
  starting transfers between devices  79.8 us (35%)
  waiting for transfers between devices  62.9 us (28%)
  local copies, waits for them, and re-layouts  47.4 us (21%)
  matrix products  20.8 us (9%)
  other arithmetic  12.5 us (6%)
    ppermute x42, starting transfers between devices, move(): return lax.ppermute(value, AXES, pairs)  79.8 us
    ppermute x42, waiting for transfers between devices, move(): return lax.ppermute(value, AXES, pairs)  62.9 us
    unnamed x44, local copies, waits for them, and re-layouts  29.2 us
    dot_general x1, matrix products, per_device(): y_send = jnp.dot(x_half, h_core, preferred_element_type=F32)  7 us
    dot_general x1, matrix products, per_device(): lax.dot_general(y, inputs, (((1,), (1,)), ((), ())), preferred_element_ty...  6.39 us
    unnamed x9, other arithmetic  6.37 us
    gather x1, local copies, waits for them, and re-layouts, per_device(): r_core = jnp.take(r_core, pick, axis=0).reshape(4096, 512)  5.06 us
    gather x1, local copies, waits for them, and re-layouts, per_device(): r_mine = jnp.take(r_mine, pick, axis=0).reshape(4096, 512)  4.99 us
  transfers between devices with their start and end apart: 42, of which 14 were waited for; matrix products, arithmetic and copies ran while one was open for 21% of the time, Pallas kernels for 0%

profile of v1, /device:TPU:0, one launch (start us, length us, event | category | flops | bytes accessed | tf_op | source)
XLA Modules:
  0.0 223.9 jit_solution(228311973240340847)
XLA Ops:
  21.3 3.3 %collective-permute-start.24 = (bf16[512,512]{1,0:T(8,128)(2,1)S(1)}, bf16[512,512]{1,0:T(8,128)(2,1)S(1)}, u32[]{:S(2)}, u32[]{:S(2)}) collective-permute-start(bf16[512,512]{1,0:T(8,128)(2,1)S(1)} %copy-done.3), channel_id=1, source_target_pairs={{0,32},{1,33},{2,34},{3,35},{4,36},{5,37},{6,38},{7,39},{8,40},{9,... | collective-permute-start | bytes 1572872 | tf_op jit(solution)/shard_map/ppermute | solution.py:29
  30.2 7.0 %collective-permute-done.24 = bf16[512,512]{1,0:T(8,128)(2,1)S(1)} collective-permute-done((bf16[512,512]{1,0:T(8,128)(2,1)S(1)}, bf16[512,512]{1,0:T(8,128)(2,1)S(1)}, u32[]{:S(2)}, u32[]{:S(2)}) %collective-permute-start.24) | collective-permute-done | bytes 524320 | tf_op jit(solution)/shard_map/ppermute | solution.py:29
  37.2 4.1 %collective-permute-start.25 = (bf16[512,512]{1,0:T(8,128)(2,1)S(1)}, bf16[512,512]{1,0:T(8,128)(2,1)S(1)}, u32[]{:S(2)}, u32[]{:S(2)}) collective-permute-start(bf16[512,512]{1,0:T(8,128)(2,1)S(1)} %collective-permute-done.24), channel_id=1, source_target_pairs={{0,24},{1,25},{2,26},{3,27},{4,28},{5,29},{6,30},{7,31},{8,0},{9,1... | collective-permute-start | bytes 1572872 | tf_op jit(solution)/shard_map/ppermute | solution.py:29
  41.6 3.3 %collective-permute-start.23 = (bf16[256,512]{1,0:T(8,128)(2,1)S(1)}, bf16[256,512]{1,0:T(8,128)(2,1)S(1)}, u32[]{:S(2)}, u32[]{:S(2)}) collective-permute-start(bf16[256,512]{1,0:T(8,128)(2,1)S(1)} %slice.86), channel_id=1, source_target_pairs={{0,24},{1,25},{2,26},{3,27},{4,28},{5,29},{6,30},{7,31},{8,0},{9,1... | collective-permute-start | bytes 786440 | tf_op jit(solution)/shard_map/ppermute | solution.py:29
  44.9 5.4 %collective-permute-start.1 = (bf16[512,512]{1,0:T(8,128)(2,1)}, bf16[512,512]{1,0:T(8,128)(2,1)}, u32[]{:S(2)}, u32[]{:S(2)}) collective-permute-start(bf16[512,512]{1,0:T(8,128)(2,1)} %collective-permute-done), channel_id=1, source_target_pairs={{0,0},{1,3},{2,2},{3,1},{4,4},{5,7},{6,6},{7,5},{8,9},{9,8},{10,11... | collective-permute-start | bytes 1572872 | tf_op jit(solution)/shard_map/ppermute | solution.py:29
  50.4 5.9 %collective-permute-start.28 = (bf16[512,512]{1,0:T(8,128)(2,1)S(1)}, bf16[512,512]{1,0:T(8,128)(2,1)S(1)}, u32[]{:S(2)}, u32[]{:S(2)}) collective-permute-start(bf16[512,512]{1,0:T(8,128)(2,1)S(1)} %collective-permute-done.24), channel_id=1, source_target_pairs={{0,8},{1,9},{2,10},{3,11},{4,12},{5,13},{6,14},{7,15},{8,16},{9,17... | collective-permute-start | bytes 1572872 | tf_op jit(solution)/shard_map/ppermute | solution.py:29
  57.9 3.2 %collective-permute-start.26 = (bf16[256,512]{1,0:T(8,128)(2,1)S(1)}, bf16[256,512]{1,0:T(8,128)(2,1)S(1)}, u32[]{:S(2)}, u32[]{:S(2)}) collective-permute-start(bf16[256,512]{1,0:T(8,128)(2,1)S(1)} %collective-permute-done.22), channel_id=1, source_target_pairs={{0,32},{1,33},{2,34},{3,35},{4,36},{5,37},{6,38},{7,39},{8,40},{9,... | collective-permute-start | bytes 786440 | tf_op jit(solution)/shard_map/ppermute | solution.py:29
  61.9 6.8 %collective-permute-done.26 = bf16[256,512]{1,0:T(8,128)(2,1)S(1)} collective-permute-done((bf16[256,512]{1,0:T(8,128)(2,1)S(1)}, bf16[256,512]{1,0:T(8,128)(2,1)S(1)}, u32[]{:S(2)}, u32[]{:S(2)}) %collective-permute-start.26) | collective-permute-done | bytes 262176 | tf_op jit(solution)/shard_map/ppermute | solution.py:29
  68.6 13.4 %collective-permute-start.11 = (bf16[528,512]{1,0:T(8,128)(2,1)S(1)}, bf16[528,512]{1,0:T(8,128)(2,1)S(1)}, u32[]{:S(2)}, u32[]{:S(2)}) collective-permute-start(bf16[528,512]{1,0:T(8,128)(2,1)S(1)} %pad_maximum_fusion.2), channel_id=1, source_target_pairs={{0,3},{1,0},{2,1},{3,2},{4,7},{5,4},{6,5},{7,6},{8,11},{9,8},{10,9... | collective-permute-start | bytes 1622024 | tf_op jit(solution)/shard_map/ppermute | solution.py:29
  84.0 7.0 %fusion.37 = f32[512,512]{1,0:T(8,128)} fusion(bf16[512,4096]{1,0:T(8,128)(2,1)S(1)} %constant_dynamic-update-slice_fusion, bf16[4096,512]{1,0:T(8,128)(2,1)} %collective-permute-done.29), kind=kOutput, calls=%fused_computation.105 | convolution fusion | flops 2147483648 | bytes 9437184 | tf_op jit(solution)/shard_map/dot_general | solution.py:105
  96.6 8.9 %collective-permute-done.2 = bf16[512,512]{1,0:T(8,128)(2,1)S(1)} collective-permute-done((bf16[512,512]{1,0:T(8,128)(2,1)}, bf16[512,512]{1,0:T(8,128)(2,1)S(1)}, u32[]{:S(2)}, u32[]{:S(2)}) %collective-permute-start.2) | collective-permute-done | bytes 524320 | tf_op jit(solution)/shard_map/ppermute | solution.py:29
  111.8 6.4 %fusion.25 = f32[512,512]{1,0:T(8,128)S(1)} fusion(bf16[512,512]{1,0:T(8,128)(2,1)} %param.6, f32[512,512]{1,0:T(8,128)} %collective-permute-done.30, bf16[512,4096]{1,0:T(8,128)(2,1)} %copy-done.4, bf16[4096,512]{1,0:T(8,128)(2,1)} %get-tuple-element.10), kind=kOutput, calls=%fused_computation.25 | convolution fusion | flops 2416443392 | bytes 11010048 | tf_op jit(solution)/shard_map/dot_general | solution.py:107
  121.3 3.3 %collective-permute-start.32 = (bf16[256,256]{1,0:T(8,128)(2,1)S(1)}, bf16[256,256]{1,0:T(8,128)(2,1)S(1)}, u32[]{:S(2)}, u32[]{:S(2)}) collective-permute-start(bf16[256,256]{1,0:T(8,128)(2,1)S(1)} %get-tuple-element.8), channel_id=1, source_target_pairs={{0,32},{1,33},{2,34},{3,35},{4,36},{5,37},{6,38},{7,39},{8,40},{9,... | collective-permute-start | bytes 393224 | tf_op jit(solution)/shard_map/ppermute | solution.py:29
  128.8 3.2 %collective-permute-start.9 = (bf16[256,512]{1,0:T(8,128)(2,1)}, bf16[256,512]{1,0:T(8,128)(2,1)S(1)}, u32[]{:S(2)}, u32[]{:S(2)}) collective-permute-start(bf16[256,512]{1,0:T(8,128)(2,1)} %collective-permute-done.5), channel_id=1, source_target_pairs={{0,32},{1,33},{2,34},{3,35},{4,36},{5,37},{6,38},{7,39},{8,40},{9,... | collective-permute-start | bytes 786440 | tf_op jit(solution)/shard_map/ppermute | solution.py:29
  134.2 4.1 %collective-permute-done.9 = bf16[256,512]{1,0:T(8,128)(2,1)S(1)} collective-permute-done((bf16[256,512]{1,0:T(8,128)(2,1)}, bf16[256,512]{1,0:T(8,128)(2,1)S(1)}, u32[]{:S(2)}, u32[]{:S(2)}) %collective-permute-start.9) | collective-permute-done | bytes 262176 | tf_op jit(solution)/shard_map/ppermute | solution.py:29
  141.8 3.2 %collective-permute-start.34 = (bf16[256,256]{1,0:T(8,128)(2,1)S(1)}, bf16[256,256]{1,0:T(8,128)(2,1)S(1)}, u32[]{:S(2)}, u32[]{:S(2)}) collective-permute-start(bf16[256,256]{1,0:T(8,128)(2,1)S(1)} %fusion.32), channel_id=1, source_target_pairs={{0,24},{1,25},{2,26},{3,27},{4,28},{5,29},{6,30},{7,31},{8,16},{9,... | collective-permute-start | bytes 393224 | tf_op jit(solution)/shard_map/ppermute | solution.py:29
  151.5 4.0 %collective-permute-start.16 = (bf16[528,512]{1,0:T(8,128)(2,1)}, bf16[528,512]{1,0:T(8,128)(2,1)S(1)}, u32[]{:S(2)}, u32[]{:S(2)}) collective-permute-start(bf16[528,512]{1,0:T(8,128)(2,1)} %collective-permute-done.15), channel_id=1, source_target_pairs={{0,3},{1,0},{2,1},{3,2},{4,7},{5,4},{6,5},{7,6},{8,11},{9,8},{10,9... | collective-permute-start | bytes 1622024 | tf_op jit(solution)/shard_map/ppermute | solution.py:29
  161.8 3.1 %collective-permute-start.36 = (bf16[2,256,256]{2,1,0:T(8,128)(2,1)S(1)}, bf16[2,256,256]{2,1,0:T(8,128)(2,1)S(1)}, u32[]{:S(2)}, u32[]{:S(2)}) collective-permute-start(bf16[2,256,256]{2,1,0:T(8,128)(2,1)S(1)} %pad_maximum_fusion.3), channel_id=1, source_target_pairs={{0,3},{1,0},{2,1},{3,2},{4,7},{5,4},{6,5},{7,6},{8,11},{9,8},{10,9... | collective-permute-start | bytes 786440 | tf_op jit(solution)/shard_map/ppermute | solution.py:29
  165.7 12.9 %collective-permute-done.37 = bf16[2,256,256]{2,1,0:T(8,128)(2,1)S(1)} collective-permute-done((bf16[2,256,256]{2,1,0:T(8,128)(2,1)S(1)}, bf16[2,256,256]{2,1,0:T(8,128)(2,1)S(1)}, u32[]{:S(2)}, u32[]{:S(2)}) %collective-permute-start.37) | collective-permute-done | bytes 262176 | tf_op jit(solution)/shard_map/ppermute | solution.py:29
  180.3 6.1 %collective-permute-done.38 = bf16[256,256]{1,0:T(8,128)(2,1)S(1)} collective-permute-done((bf16[256,256]{1,0:T(8,128)(2,1)S(1)}, bf16[256,256]{1,0:T(8,128)(2,1)S(1)}, u32[]{:S(2)}, u32[]{:S(2)}) %collective-permute-start.38) | collective-permute-done | bytes 131104 | tf_op jit(solution)/shard_map/ppermute | solution.py:29
  188.5 3.1 %collective-permute-done.39 = bf16[256,256]{1,0:T(8,128)(2,1)S(1)} collective-permute-done((bf16[256,256]{1,0:T(8,128)(2,1)S(1)}, bf16[256,256]{1,0:T(8,128)(2,1)S(1)}, u32[]{:S(2)}, u32[]{:S(2)}) %collective-permute-start.39) | collective-permute-done | bytes 131104 | tf_op jit(solution)/shard_map/ppermute | solution.py:29
  193.3 4.8 %collective-permute-done.18 = bf16[272,512]{1,0:T(8,128)(2,1)S(1)} collective-permute-done((bf16[272,512]{1,0:T(8,128)(2,1)S(1)}, bf16[272,512]{1,0:T(8,128)(2,1)S(1)}, u32[]{:S(2)}, u32[]{:S(2)}) %collective-permute-start.18) | collective-permute-done | bytes 278560 | tf_op jit(solution)/shard_map/ppermute | solution.py:29
  202.1 5.0 %gather_fusion = bf16[8,512,512]{2,1,0:T(8,128)(2,1)} fusion(bf16[8,512,512]{2,1,0:T(8,128)(2,1)} %bitcast_dynamic-update-slice_fusion.6, s32[1024]{0:T(1024)S(1)} %pad_clamp_fusion), kind=kCustom, calls=%fused_computation.clone | custom fusion | bytes 8388640 | tf_op jit(solution)/shard_map/jit(_take)/gather | solution.py:150
  207.1 5.1 %gather_fusion.1 = bf16[8,512,512]{2,1,0:T(8,128)(2,1)} fusion(bf16[8,512,512]{2,1,0:T(8,128)(2,1)} %collective-permute-done.41, s32[1024]{0:T(1024)S(1)} %pad_clamp_fusion), kind=kCustom, calls=%fused_computation.1.clone | custom fusion | bytes 8388640 | tf_op jit(solution)/shard_map/jit(_take)/gather | solution.py:151
  (153 shorter events, 90.7 us)
Async XLA Ops:
  21.3 62.6 %collective-permute-start.29 = (bf16[4096,512]{1,0:T(8,128)(2,1)}, bf16[4096,512]{1,0:T(8,128)(2,1)}, u32[]{:S(2)}, u32[]{:S(2)}) collective-permute-start(bf16[4096,512]{1,0:T(8,128)(2,1)} %dynamic-slice_dynamic-update-slice_fusion), channel_id=1, source_target_pairs={{0,4},{1,5},{2,6},{3,7},{4,0},{5,1},{6,2},{7,3},{8,12},{9,13},{10,... | collective-permute-start | bytes 12582920 | tf_op jit(solution)/shard_map/ppermute | solution.py:29
  21.3 15.9 %collective-permute-start.24 = (bf16[512,512]{1,0:T(8,128)(2,1)S(1)}, bf16[512,512]{1,0:T(8,128)(2,1)S(1)}, u32[]{:S(2)}, u32[]{:S(2)}) collective-permute-start(bf16[512,512]{1,0:T(8,128)(2,1)S(1)} %copy-done.3), channel_id=1, source_target_pairs={{0,32},{1,33},{2,34},{3,35},{4,36},{5,37},{6,38},{7,39},{8,40},{9,... | collective-permute-start | bytes 1572872 | tf_op jit(solution)/shard_map/ppermute | solution.py:29
  24.6 16.8 %collective-permute-start.21 = (bf16[512,512]{1,0:T(8,128)(2,1)S(1)}, bf16[512,512]{1,0:T(8,128)(2,1)S(1)}, u32[]{:S(2)}, u32[]{:S(2)}) collective-permute-start(bf16[512,512]{1,0:T(8,128)(2,1)S(1)} %copy-done.3), channel_id=1, source_target_pairs={{0,8},{1,9},{2,10},{3,11},{4,12},{5,13},{6,14},{7,15},{8,16},{9,17... | collective-permute-start | bytes 1572872 | tf_op jit(solution)/shard_map/ppermute | solution.py:29
  26.6 15.0 %collective-permute-start.20 = (bf16[512,512]{1,0:T(8,128)(2,1)S(1)}, bf16[512,512]{1,0:T(8,128)(2,1)S(1)}, u32[]{:S(2)}, u32[]{:S(2)}) collective-permute-start(bf16[512,512]{1,0:T(8,128)(2,1)S(1)} %copy-done.3), channel_id=1, source_target_pairs={{0,24},{1,25},{2,26},{3,27},{4,28},{5,29},{6,30},{7,31},{8,0},{9,1... | collective-permute-start | bytes 1572872 | tf_op jit(solution)/shard_map/ppermute | solution.py:29
  28.7 16.2 %collective-permute-start = (bf16[512,512]{1,0:T(8,128)(2,1)S(1)}, bf16[512,512]{1,0:T(8,128)(2,1)}, u32[]{:S(2)}, u32[]{:S(2)}) collective-permute-start(bf16[512,512]{1,0:T(8,128)(2,1)S(1)} %copy-done.2), channel_id=1, source_target_pairs={{0,0},{1,9},{2,18},{3,27},{4,4},{5,13},{6,22},{7,31},{8,8},{9,17},... | collective-permute-start | bytes 1572872 | tf_op jit(solution)/shard_map/ppermute | solution.py:29
  37.2 24.0 %collective-permute-start.25 = (bf16[512,512]{1,0:T(8,128)(2,1)S(1)}, bf16[512,512]{1,0:T(8,128)(2,1)S(1)}, u32[]{:S(2)}, u32[]{:S(2)}) collective-permute-start(bf16[512,512]{1,0:T(8,128)(2,1)S(1)} %collective-permute-done.24), channel_id=1, source_target_pairs={{0,24},{1,25},{2,26},{3,27},{4,28},{5,29},{6,30},{7,31},{8,0},{9,1... | collective-permute-start | bytes 1572872 | tf_op jit(solution)/shard_map/ppermute | solution.py:29
  41.6 16.4 %collective-permute-start.23 = (bf16[256,512]{1,0:T(8,128)(2,1)S(1)}, bf16[256,512]{1,0:T(8,128)(2,1)S(1)}, u32[]{:S(2)}, u32[]{:S(2)}) collective-permute-start(bf16[256,512]{1,0:T(8,128)(2,1)S(1)} %slice.86), channel_id=1, source_target_pairs={{0,24},{1,25},{2,26},{3,27},{4,28},{5,29},{6,30},{7,31},{8,0},{9,1... | collective-permute-start | bytes 786440 | tf_op jit(solution)/shard_map/ppermute | solution.py:29
  44.9 37.1 %collective-permute-start.1 = (bf16[512,512]{1,0:T(8,128)(2,1)}, bf16[512,512]{1,0:T(8,128)(2,1)}, u32[]{:S(2)}, u32[]{:S(2)}) collective-permute-start(bf16[512,512]{1,0:T(8,128)(2,1)} %collective-permute-done), channel_id=1, source_target_pairs={{0,0},{1,3},{2,2},{3,1},{4,4},{5,7},{6,6},{7,5},{8,9},{9,8},{10,11... | collective-permute-start | bytes 1572872 | tf_op jit(solution)/shard_map/ppermute | solution.py:29
  50.4 33.5 %collective-permute-start.28 = (bf16[512,512]{1,0:T(8,128)(2,1)S(1)}, bf16[512,512]{1,0:T(8,128)(2,1)S(1)}, u32[]{:S(2)}, u32[]{:S(2)}) collective-permute-start(bf16[512,512]{1,0:T(8,128)(2,1)S(1)} %collective-permute-done.24), channel_id=1, source_target_pairs={{0,8},{1,9},{2,10},{3,11},{4,12},{5,13},{6,14},{7,15},{8,16},{9,17... | collective-permute-start | bytes 1572872 | tf_op jit(solution)/shard_map/ppermute | solution.py:29
  61.2 22.6 %collective-permute-start.27 = (bf16[256,512]{1,0:T(8,128)(2,1)S(1)}, bf16[256,512]{1,0:T(8,128)(2,1)S(1)}, u32[]{:S(2)}, u32[]{:S(2)}) collective-permute-start(bf16[256,512]{1,0:T(8,128)(2,1)S(1)} %collective-permute-done.23), channel_id=1, source_target_pairs={{0,32},{1,33},{2,34},{3,35},{4,36},{5,37},{6,38},{7,39},{8,40},{9,... | collective-permute-start | bytes 786440 | tf_op jit(solution)/shard_map/ppermute | solution.py:29
  68.6 78.3 %collective-permute-start.11 = (bf16[528,512]{1,0:T(8,128)(2,1)S(1)}, bf16[528,512]{1,0:T(8,128)(2,1)S(1)}, u32[]{:S(2)}, u32[]{:S(2)}) collective-permute-start(bf16[528,512]{1,0:T(8,128)(2,1)S(1)} %pad_maximum_fusion.2), channel_id=1, source_target_pairs={{0,3},{1,0},{2,1},{3,2},{4,7},{5,4},{6,5},{7,6},{8,11},{9,8},{10,9... | collective-permute-start | bytes 1622024 | tf_op jit(solution)/shard_map/ppermute | solution.py:29
  91.0 20.4 %collective-permute-start.30 = (f32[512,512]{1,0:T(8,128)}, f32[512,512]{1,0:T(8,128)}, u32[]{:S(2)}, u32[]{:S(2)}) collective-permute-start(f32[512,512]{1,0:T(8,128)} %fusion.37), channel_id=1, source_target_pairs={{0,4},{1,5},{2,6},{3,7},{4,0},{5,1},{6,2},{7,3},{8,12},{9,13},{10,... | collective-permute-start | bytes 3145736 | tf_op jit(solution)/shard_map/ppermute | solution.py:29
  92.8 15.8 %collective-permute-start.6 = (bf16[512,512]{1,0:T(8,128)(2,1)}, bf16[512,512]{1,0:T(8,128)(2,1)}, u32[]{:S(2)}, u32[]{:S(2)}) collective-permute-start(bf16[512,512]{1,0:T(8,128)(2,1)} %collective-permute-done.1), channel_id=1, source_target_pairs={{0,32},{1,33},{2,34},{3,35},{4,36},{5,37},{6,38},{7,39},{8,40},{9,... | collective-permute-start | bytes 1572872 | tf_op jit(solution)/shard_map/ppermute | solution.py:29
  94.7 16.7 %collective-permute-start.4 = (bf16[256,512]{1,0:T(8,128)(2,1)S(1)}, bf16[256,512]{1,0:T(8,128)(2,1)S(1)}, u32[]{:S(2)}, u32[]{:S(2)}) collective-permute-start(bf16[256,512]{1,0:T(8,128)(2,1)S(1)} %slice.78), channel_id=1, source_target_pairs={{0,8},{1,9},{2,10},{3,11},{4,12},{5,13},{6,14},{7,15},{8,16},{9,17... | collective-permute-start | bytes 786440 | tf_op jit(solution)/shard_map/ppermute | solution.py:29
  108.6 23.5 %collective-permute-start.7 = (bf16[512,512]{1,0:T(8,128)(2,1)}, bf16[512,512]{1,0:T(8,128)(2,1)}, u32[]{:S(2)}, u32[]{:S(2)}) collective-permute-start(bf16[512,512]{1,0:T(8,128)(2,1)} %collective-permute-done.6), channel_id=1, source_target_pairs={{0,24},{1,25},{2,26},{3,27},{4,28},{5,29},{6,30},{7,31},{8,0},{9,1... | collective-permute-start | bytes 1572872 | tf_op jit(solution)/shard_map/ppermute | solution.py:29
  111.4 33.6 %collective-permute-start.10 = (bf16[512,512]{1,0:T(8,128)(2,1)}, bf16[512,512]{1,0:T(8,128)(2,1)}, u32[]{:S(2)}, u32[]{:S(2)}) collective-permute-start(bf16[512,512]{1,0:T(8,128)(2,1)} %collective-permute-done.6), channel_id=1, source_target_pairs={{0,8},{1,9},{2,10},{3,11},{4,12},{5,13},{6,14},{7,15},{8,16},{9,17... | collective-permute-start | bytes 1572872 | tf_op jit(solution)/shard_map/ppermute | solution.py:29
  111.4 22.8 %collective-permute-start.8 = (bf16[256,512]{1,0:T(8,128)(2,1)S(1)}, bf16[256,512]{1,0:T(8,128)(2,1)}, u32[]{:S(2)}, u32[]{:S(2)}) collective-permute-start(bf16[256,512]{1,0:T(8,128)(2,1)S(1)} %collective-permute-done.4), channel_id=1, source_target_pairs={{0,32},{1,33},{2,34},{3,35},{4,36},{5,37},{6,38},{7,39},{8,40},{9,... | collective-permute-start | bytes 786440 | tf_op jit(solution)/shard_map/ppermute | solution.py:29
  134.2 15.6 %collective-permute-start.12 = (bf16[528,512]{1,0:T(8,128)(2,1)S(1)}, bf16[528,512]{1,0:T(8,128)(2,1)S(1)}, u32[]{:S(2)}, u32[]{:S(2)}) collective-permute-start(bf16[528,512]{1,0:T(8,128)(2,1)S(1)} %pad_maximum_fusion.2), channel_id=1, source_target_pairs={{0,1},{1,2},{2,3},{3,0},{4,5},{5,6},{6,7},{7,4},{8,9},{9,10},{10,1... | collective-permute-start | bytes 1622024 | tf_op jit(solution)/shard_map/ppermute | solution.py:29
  146.9 60.2 %collective-permute-start.41 = (bf16[8,512,512]{2,1,0:T(8,128)(2,1)}, bf16[8,512,512]{2,1,0:T(8,128)(2,1)}, u32[]{:S(2)}, u32[]{:S(2)}) collective-permute-start(bf16[8,512,512]{2,1,0:T(8,128)(2,1)} %bitcast_dynamic-update-slice_fusion.6), channel_id=1, source_target_pairs={{0,4},{1,5},{2,6},{3,7},{4,0},{5,1},{6,2},{7,3},{8,12},{9,13},{10,... | collective-permute-start | bytes 12582920 | tf_op jit(solution)/shard_map/ppermute | solution.py:29
  151.5 40.6 %collective-permute-start.16 = (bf16[528,512]{1,0:T(8,128)(2,1)}, bf16[528,512]{1,0:T(8,128)(2,1)S(1)}, u32[]{:S(2)}, u32[]{:S(2)}) collective-permute-start(bf16[528,512]{1,0:T(8,128)(2,1)} %collective-permute-done.15), channel_id=1, source_target_pairs={{0,3},{1,0},{2,1},{3,2},{4,7},{5,4},{6,5},{7,6},{8,11},{9,8},{10,9... | collective-permute-start | bytes 1622024 | tf_op jit(solution)/shard_map/ppermute | solution.py:29
  160.6 38.4 %collective-permute-start.19 = (bf16[528,512]{1,0:T(8,128)(2,1)}, bf16[528,512]{1,0:T(8,128)(2,1)S(1)}, u32[]{:S(2)}, u32[]{:S(2)}) collective-permute-start(bf16[528,512]{1,0:T(8,128)(2,1)} %collective-permute-done.15), channel_id=1, source_target_pairs={{0,1},{1,2},{2,3},{3,0},{4,5},{5,6},{6,7},{7,4},{8,9},{9,10},{10,1... | collective-permute-start | bytes 1622024 | tf_op jit(solution)/shard_map/ppermute | solution.py:29
  160.7 18.0 %collective-permute-start.37 = (bf16[2,256,256]{2,1,0:T(8,128)(2,1)S(1)}, bf16[2,256,256]{2,1,0:T(8,128)(2,1)S(1)}, u32[]{:S(2)}, u32[]{:S(2)}) collective-permute-start(bf16[2,256,256]{2,1,0:T(8,128)(2,1)S(1)} %pad_maximum_fusion.3), channel_id=1, source_target_pairs={{0,1},{1,2},{2,3},{3,0},{4,5},{5,6},{6,7},{7,4},{8,9},{9,10},{10,1... | collective-permute-start | bytes 786440 | tf_op jit(solution)/shard_map/ppermute | solution.py:29
  161.8 18.4 %collective-permute-start.36 = (bf16[2,256,256]{2,1,0:T(8,128)(2,1)S(1)}, bf16[2,256,256]{2,1,0:T(8,128)(2,1)S(1)}, u32[]{:S(2)}, u32[]{:S(2)}) collective-permute-start(bf16[2,256,256]{2,1,0:T(8,128)(2,1)S(1)} %pad_maximum_fusion.3), channel_id=1, source_target_pairs={{0,3},{1,0},{2,1},{3,2},{4,7},{5,4},{6,5},{7,6},{8,11},{9,8},{10,9... | collective-permute-start | bytes 786440 | tf_op jit(solution)/shard_map/ppermute | solution.py:29
  192.1 20.1 %collective-permute-start.40 = (bf16[8,256,256]{2,1,0:T(8,128)(2,1)S(1)}, bf16[8,256,256]{2,1,0:T(8,128)(2,1)}, u32[]{:S(2)}, u32[]{:S(2)}) collective-permute-start(bf16[8,256,256]{2,1,0:T(8,128)(2,1)S(1)} %slice_dynamic-update-slice_fusion), channel_id=1, source_target_pairs={{0,4},{1,5},{2,6},{3,7},{4,0},{5,1},{6,2},{7,3},{8,12},{9,13},{10,... | collective-permute-start | bytes 3145736 | tf_op jit(solution)/shard_map/ppermute | solution.py:29
  (26 other events, 255.2 us)

commit v2 on v1

v2 whole, which is shorter than its diff:
```python
import functools

import jax
import jax.numpy as jnp
from jax import lax
from jax.experimental import pallas as pl
from jax.experimental.pallas import tpu as pltpu
from jax.sharding import Mesh, PartitionSpec as P


AXES = ("yl", "yh", "z", "k", "x")
SIZES = (2, 2, 4, 2, 4)

F32 = jnp.float32
BF16 = jnp.bfloat16


def linear(place):
    index = 0
    for part, size in zip(place, SIZES):
        index = index * size + part
    return index


def place_of(index):
    parts = []
    for size in reversed(SIZES):
        parts.append(index % size)
        index //= size
    return tuple(reversed(parts))


def move(value, where):
    pairs = [(i, linear(where(*place_of(i)))) for i in range(128)]
    return lax.ppermute(value, AXES, pairs)


def z_up(yl, yh, z, k, x):
    return yl, yh, (z + 1) % 4, k, x


def z_down(yl, yh, z, k, x):
    return yl, yh, (z - 1) % 4, k, x


def x_up(yl, yh, z, k, x):
    return yl, yh, z, k, (x + 1) % 4


def x_down(yl, yh, z, k, x):
    return yl, yh, z, k, (x - 1) % 4


def swap_yh(yl, yh, z, k, x):
    return yl, 1 - yh, z, k, x


def swap_yl(yl, yh, z, k, x):
    return 1 - yl, yh, z, k, x


def swap_core(yl, yh, z, k, x):
    return yl, yh, z, 1 - k, x


def z_pair_a(yl, yh, z, k, x):
    return yl, yh, z ^ 1, k, x


def z_pair_b(yl, yh, z, k, x):
    return yl, yh, (z + 1 if z % 2 else z - 1) % 4, k, x


def shear(yl, yh, z, k, x):
    return yl, yh, (z + x) % 4, k, x


def reflect(yl, yh, z, k, x):
    return yh, yl, z, k, (z - x) % 4


def z_far(yl, yh, z, k, x):
    return yl, yh, (z + 2) % 4, k, x


def x_far(yl, yh, z, k, x):
    return yl, yh, z, k, (x + 2) % 4


def gather(own, up, down, two, across, cut):
    below = move(own, up)
    above = move(own, down)
    over = move(own, across)
    over_below = move(over, up)
    over_above = move(over, down)
    if cut is None:
        far = (move(own, two),)
        over_far = (move(far[0], across),)
    else:
        far = (move(below[:cut], up), move(above[cut:], down))
        over_far = (move(far[0], across), move(far[1], across))
    return [own, above, far, below, over, over_above, over_far, over_below]


VMEM = pl.BlockSpec(memory_space=pltpu.VMEM)
HBM = pl.BlockSpec(memory_space=pltpu.HBM)
ANY = pl.BlockSpec(memory_space=pl.ANY)
SMEM = pl.BlockSpec(memory_space=pltpu.SMEM)
MIB = 1 << 20


def cut_body(core, mine, other, out):
    rows = pl.ds(pl.multiple_of(core[0] * 256, 256), 256)
    out[:, :512] = mine[rows, :]
    out[:, 512:] = other[rows, :]


def cut_rows(core, mine, other):
    return pl.pallas_call(
        cut_body,
        out_shape=jax.ShapeDtypeStruct((256, 1024), BF16),
        in_specs=[SMEM, VMEM, VMEM],
        out_specs=VMEM,
        compiler_params=pltpu.CompilerParams(vmem_limit_bytes=4 * MIB),
        cost_estimate=pl.CostEstimate(flops=0, bytes_accessed=MIB, transcendentals=0),
        name="cut_rows",
    )(core, mine, other)


def documents(marked, held):
    columns = jnp.transpose(marked[512:528, :].astype(F32))
    held[...] = jnp.broadcast_to(columns[:, :1], (512, 128))
    return marked[512:513, :].astype(F32)


def y_body(parts, first, last, where, *refs):
    n = len(parts)
    xs = []
    for count in parts:
        xs.append(refs[:count])
        refs = refs[count:]
    h, h_core, refs = refs[0], refs[1], refs[2:]
    if first:
        before = (None, None)
    else:
        before, refs = refs[:2], refs[2:]
    if last:
        x_mine, x_core, marked, folded, sum_mine, sum_core, column, held, sem = refs
        sums = (sum_mine, sum_core)
    else:
        sums, (held, sem) = refs[:2], refs[2:]
    k = where[n]

    def copies(j):
        for t, source in enumerate((h, h_core)):
            for i, part in enumerate((k, 1 - k)):
                row = pl.multiple_of(where[j] * 1024 + part * 512, 512)
                yield pltpu.make_async_copy(
                    source.at[pl.ds(row, 512), :],
                    held.at[j, t, pl.ds(i * 512, 512), :],
                    sem.at[j, t, i],
                )

    for j in range(n):
        for copy in copies(j):
            copy.start()
    for j in range(n):
        for copy in copies(j):
            copy.wait()
        at = 0
        for x in xs[j]:
            rows = slice(at, at + x.shape[0])
            at += x.shape[0]
            for t, (old, new) in enumerate(zip(before, sums)):
                term = jnp.dot(x[...], held[j, t], preferred_element_type=F32)
                if j > 0:
                    new[rows] += term
                elif first:
                    new[rows] = term
                else:
                    new[rows] = old[rows] + term
    if last:
        p = sum(
            lax.dot_general(
                y[...].astype(BF16), x[...], (((1,), (1,)), ((), ())), preferred_element_type=F32
            )
            for y, x in zip(sums, (x_mine, x_core))
        )
        row = documents(marked, column)
        tokens = column[pl.ds(pl.multiple_of(k * 256, 256), 256), :][:, :1]
        folded[...] = jnp.where(
            tokens == row[:, :256], p[:, :256], jnp.where(tokens == row[:, 256:], p[:, 256:], 0.0)
        )


def y_stage(xs, where, h, h_core, before, final=None):
    n = len(xs)
    first = before is None
    before = () if first else before
    xs = [x if isinstance(x, tuple) else (x,) for x in xs]
    parts = tuple(len(x) for x in xs)
    xs = [piece for x in xs for piece in x]
    last = final is not None
    if last:
        out_shape = [jax.ShapeDtypeStruct((256, 256), F32)]
        more = [pltpu.VMEM((256, 512), F32)] * 2 + [pltpu.VMEM((512, 128), F32)]
    else:
        out_shape = [jax.ShapeDtypeStruct((256, 512), F32)] * 2
        more = []
    final = final if last else ()
    return pl.pallas_call(
        functools.partial(y_body, parts, first, last),
        out_shape=out_shape,
        in_specs=[SMEM] + [VMEM] * len(xs) + [HBM, HBM] + [VMEM] * (len(before) + len(final)),
        out_specs=[VMEM] * len(out_shape),
        scratch_shapes=more
        + [pltpu.VMEM((n, 2, 1024, 512), BF16), pltpu.SemaphoreType.DMA((n, 2, 2))],
        compiler_params=pltpu.CompilerParams(vmem_limit_bytes=24 * MIB),
        cost_estimate=pl.CostEstimate(
            flops=n * (1 << 29), bytes_accessed=n * 2 * MIB + 2 * MIB, transcendentals=0
        ),
        name="y_stage",
    )(where, *xs, h, h_core, *before, *final)


def z_body(ks, core, *refs):
    parts, refs = refs[: len(ks)], refs[len(ks) :]
    n = sum(ks)
    mine, other, (out, column) = refs[:n], refs[n : 2 * n], refs[2 * n :]
    rows = pl.ds(pl.multiple_of(core[0] * 256, 256), 256)
    blocks = [part[i, ...] for part, count in zip(parts, ks) for i in range(count)]
    for i in range(n):
        row = documents(mine[i], column)
        low = jnp.where(column[rows, :][:, :1] == row[:, :256], blocks[i], jnp.zeros((), BF16))
        high = blocks[i] - low
        for t, d in enumerate((mine[i], other[i])):
            out[i, :, t * 512 : (t + 1) * 512] = (
                jnp.dot(low, d[:256], preferred_element_type=F32)
                + jnp.dot(high, d[256:512], preferred_element_type=F32)
            ).astype(BF16)


def z_stage(core, parts, mine, other):
    n = len(mine)
    return pl.pallas_call(
        functools.partial(z_body, tuple(part.shape[0] for part in parts)),
        out_shape=jax.ShapeDtypeStruct((n, 256, 1024), BF16),
        in_specs=[SMEM] + [VMEM] * (len(parts) + 2 * n),
        out_specs=VMEM,
        scratch_shapes=[pltpu.VMEM((512, 128), F32)],
        compiler_params=pltpu.CompilerParams(vmem_limit_bytes=24 * MIB),
        cost_estimate=pl.CostEstimate(
            flops=n * (1 << 28), bytes_accessed=n * 2 * MIB, transcendentals=0
        ),
        name="z_stage",
    )(core, *parts, *mine, *other)


def out_body(counts, sides, first, core, *refs):
    n = len(counts)
    rs = []
    for count in counts:
        rs.append(refs[:count])
        refs = refs[count:]
    near, far, refs = refs[0], refs[1], refs[2:]
    if not first:
        before, refs = refs[: len(sides)], refs[len(sides) :]
    outs, (held, z, sem) = refs[: len(sides)], refs[len(sides) :]
    k = core[0]
    width = 512 * len(sides)
    columns = pl.ds(sides[0] * 512, width)
    for i in range(n):
        at = i * 256
        for piece in rs[i]:
            rows = pl.ds(at, piece.shape[0])
            at += piece.shape[0]
            pltpu.make_async_copy(piece, held.at[rows], sem.at[i, 0]).start()
        place = core[1 + i]

        @pl.when(place < 2)
        def _():
            source = near.at[place, :, columns]
            pltpu.make_async_copy(source, z.at[pl.ds(i * 256, 256)], sem.at[i, 1]).start()

        @pl.when(place >= 2)
        def _():
            source = far.at[place - 2, :, columns]
            pltpu.make_async_copy(source, z.at[pl.ds(i * 256, 256)], sem.at[i, 1]).start()

    for i in range(n):
        rows = pl.ds(i * 256, 256)
        pltpu.make_async_copy(held.at[rows], held.at[rows], sem.at[i, 0]).wait()
        pltpu.make_async_copy(z.at[rows], z.at[rows], sem.at[i, 1]).wait()
    for i, part in enumerate((k, 1 - k)):
        rows = pl.ds(pl.multiple_of(part * 512, 512), 512)
        for t in range(len(sides)):
            term = lax.dot_general(
                held[:, i * 512 : (i + 1) * 512],
                z[:, t * 512 : (t + 1) * 512],
                (((0,), (0,)), ((), ())),
                preferred_element_type=F32,
            )
            outs[t][rows, :] = term if first else before[t][rows, :] + term


def out_stage(core, rs, near, far, sides, before):
    n = len(rs)
    counts = tuple(len(r) for r in rs)
    rs = [piece for r in rs for piece in r]
    return pl.pallas_call(
        functools.partial(out_body, counts, sides, not before),
        out_shape=[jax.ShapeDtypeStruct((1024, 512), F32)] * len(sides),
        in_specs=[SMEM] + [ANY] * (len(rs) + 2) + [VMEM] * len(before),
        out_specs=[VMEM] * len(sides),
        scratch_shapes=[
            pltpu.VMEM((n * 256, 1024), BF16),
            pltpu.VMEM((n * 256, 512 * len(sides)), BF16),
            pltpu.SemaphoreType.DMA((n, 2)),
        ],
        compiler_params=pltpu.CompilerParams(vmem_limit_bytes=24 * MIB),
        cost_estimate=pl.CostEstimate(
            flops=n * len(sides) * (1 << 28), bytes_accessed=n * MIB + 4 * MIB, transcendentals=0
        ),
        name="out_stage",
    )(core, *rs, near, far, *before)


EARLY = (0, 1, 3, 4)


def step(inputs, grads, h_in, segments):
    yl, yh, z, k, x = (lax.axis_index(name) for name in AXES)
    core = jnp.stack([k])

    x_core = move(inputs, swap_core)
    x_rows = cut_rows(core, inputs, x_core)
    xs = gather(x_rows, z_up, z_down, z_far, swap_yh, 128)
    h_core = move(h_in, swap_core)
    order = [(yh ^ a) * 4 + (z + b) % 4 for a in range(2) for b in range(4)]
    marked = jnp.concatenate([grads, jnp.broadcast_to(segments.astype(BF16), (16, 512))])

    sums = None
    for turn, chosen in enumerate(((0, 1, 3, 4), (2, 5, 7), (6,))):
        final = (inputs, x_core, marked) if turn == 2 else None
        where = jnp.stack([order[i] for i in chosen] + [k])
        sums = y_stage([xs[i] for i in chosen], where, h_in, h_core, sums, final)
    acc = sums[0]
    for where in (z_pair_a, z_pair_b, swap_yh):
        acc = acc + move(acc.astype(BF16), where).astype(F32)
    kh = acc.astype(BF16)
    pair = jnp.stack([kh, move(kh, swap_yl)])
    below = move(pair, x_up)
    above = move(pair, x_down)
    far = move(pair, x_far)

    ds = gather(marked, x_up, x_down, x_far, swap_yl, None)
    ds = [d[0] if isinstance(d, tuple) else d for d in ds]
    d_core = move(grads, swap_core)
    others = [d_core] + [move(ds[i], swap_core) for i in range(1, 8)]
    z_near = z_stage(core, (pair,), ds[::4], others[::4])
    chosen = (1, 5, 2, 6, 3, 7)
    z_rest = z_stage(
        core, (above, far, below), [ds[i] for i in chosen], [others[i] for i in chosen]
    )

    d_rows = cut_rows(core, grads, d_core)
    turned = move(move(d_rows, shear), reflect)
    rs = gather(turned, z_up, z_down, z_far, swap_yh, 128)
    rs = [r if isinstance(r, tuple) else (r,) for r in rs]
    places = [(z + i % 4 - 2 * x) % 4 * 2 + (yl ^ yh ^ (i // 4)) for i in range(8)]

    early, late = EARLY, [i for i in range(8) if i not in EARLY]
    pick = [jnp.stack([k] + [places[i] for i in some]) for some in (early, late)]
    blocks = [[rs[i] for i in some] for some in (early, late)]
    out_mine, out_send = out_stage(pick[0], blocks[0], z_near, z_rest, (0, 1), ())
    (out_send,) = out_stage(pick[1], blocks[1], z_near, z_rest, (1,), (out_send,))
    out_got = move(out_send, swap_core)
    (out_mine,) = out_stage(pick[1], blocks[1], z_near, z_rest, (0,), (out_mine,))
    return out_mine + out_got


def solution(mesh):
    fine = Mesh(mesh.devices.reshape(SIZES), AXES)
    col = ("yh", "z", "k")
    row = ("yl", "x")
    return jax.shard_map(
        step,
        mesh=fine,
        in_specs=(P(row, col), P(row, col), P(None, col), P(row, None)),
        out_specs=P(row, col),
        check_vma=False,
    )
```

time: 225 us -> 194 us (0.86)
  local copies, waits for them, and re-layouts: 47.4 us -> 11.6 us
  Pallas kernels: 0 us -> 28.6 us
  matrix products: 20.8 us -> 0 us
  other arithmetic: 12.5 us -> 3.92 us
  waiting for transfers between devices: 62.9 us -> 68.2 us
    pallas_call x0 -> x10, Pallas kernels: none -> 28.6 us  [the longest x3 13.5 us: y_stage(): pl.pallas_call(functools.partial(y_body, parts, first, last), out_shape=o...]
    dot_general x5 -> x0, matrix products: 20.8 us -> none  [the longest x1 7 us: per_device(): y_send = jnp.dot(x_half, h_core, preferred_element_type=F32)]
    unnamed x44 -> x56, local copies, waits for them, and re-layouts: 29.2 us -> 10.6 us
    gather x2 -> x0, local copies, waits for them, and re-layouts: 10.1 us -> none  [the longest x1 5.06 us: per_device(): r_core = jnp.take(r_core, pick, axis=0).reshape(4096, 512)]
    unnamed x9 -> x0, other arithmetic: 6.37 us -> none
    ppermute x42 -> x45, waiting for transfers between devices: 62.9 us -> 68.2 us  [move(): return lax.ppermute(value, AXES, pairs)]
    concatenate x3 -> x0, local copies, waits for them, and re-layouts: 4.28 us -> none  [the longest x1 2.28 us: per_device(): jnp.concatenate([lax.dynamic_slice(h_in, (i * 1024 + k * 512, 0), (512, 5...]
    select_n x4 -> x0, other arithmetic: 2.83 us -> none  [the longest x1 1.51 us: per_device(): first = jnp.where(k == 0, halves, other)]
  transfers between devices with their start and end apart: 42 -> 45, of which waited for: 14 -> 13; matrix products, arithmetic and copies ran while one was open for 21% -> 2% of each run, Pallas kernels for 0% -> 14%
where the time goes in v2:
time: 194 us; the launch traced here: 192 us
  starting transfers between devices  79.4 us (41%)
  waiting for transfers between devices  68.2 us (35%)
  Pallas kernels  28.6 us (15%)
  local copies, waits for them, and re-layouts  11.6 us (6%)
  other arithmetic  3.92 us (2%)
    ppermute x45, starting transfers between devices, move(): return lax.ppermute(value, AXES, pairs)  79.4 us
    ppermute x45, waiting for transfers between devices, move(): return lax.ppermute(value, AXES, pairs)  68.2 us
    pallas_call x3, Pallas kernels, y_stage(): pl.pallas_call(functools.partial(y_body, parts, first, last), out_shape=o...  13.5 us
    unnamed x56, local copies, waits for them, and re-layouts  10.6 us
    pallas_call x3, Pallas kernels, out_stage(): pl.pallas_call(functools.partial(out_body, counts, sides, not before), ou...  8.87 us
    pallas_call x2, Pallas kernels, z_stage(): pl.pallas_call(functools.partial(z_body, tuple((part.shape[0] for part in...  6.23 us
  transfers between devices with their start and end apart: 45, of which 13 were waited for; matrix products, arithmetic and copies ran while one was open for 2% of the time, Pallas kernels for 14%

profile of v2, /device:TPU:0, one launch (start us, length us, event | category | flops | bytes accessed | tf_op | source)
XLA Modules:
  0.0 192.4 jit_solution(7441367306871024872)
XLA Ops:
  7.2 6.9 %collective-permute-done.12.other.refs_7_ = bf16[512,512]{1,0:T(8,128)(2,1)S(1)} collective-permute-done((bf16[512,512]{1,0:T(8,128)(2,1)}, bf16[512,512]{1,0:T(8,128)(2,1)S(1)}, u32[]{:S(2)}, u32[]{:S(2)}) %collective-permute-start.12) | collective-permute-done | bytes 524320 | tf_op jit(solution)/shard_map/ppermute | solution.py:35
  18.1 3.3 %collective-permute-start.20 = (bf16[256,1024]{1,0:T(8,128)(2,1)S(1)}, bf16[256,1024]{1,0:T(8,128)(2,1)}, u32[]{:S(2)}, u32[]{:S(2)}) collective-permute-start(bf16[256,1024]{1,0:T(8,128)(2,1)S(1)} %cut_rows.3.refs_0_), channel_id=1, source_target_pairs={{0,32},{1,33},{2,34},{3,35},{4,36},{5,37},{6,38},{7,39},{8,40},{9,... | collective-permute-start | bytes 1572872 | tf_op jit(solution)/shard_map/ppermute | solution.py:35
  23.3 8.5 %collective-permute-done.32.refs_3_ = bf16[528,512]{1,0:T(8,128)(2,1)} collective-permute-done((bf16[528,512]{1,0:T(8,128)(2,1)S(1)}, bf16[528,512]{1,0:T(8,128)(2,1)}, u32[]{:S(2)}, u32[]{:S(2)}) %collective-permute-start.32) | collective-permute-done | bytes 540704 | tf_op jit(solution)/shard_map/ppermute | solution.py:35
  31.8 4.0 %collective-permute-start.16 = (bf16[256,1024]{1,0:T(8,128)(2,1)S(1)}, bf16[256,1024]{1,0:T(8,128)(2,1)S(1)}, u32[]{:S(2)}, u32[]{:S(2)}) collective-permute-start(bf16[256,1024]{1,0:T(8,128)(2,1)S(1)} %cut_rows.3.refs_0_), channel_id=1, source_target_pairs={{0,24},{1,25},{2,26},{3,27},{4,28},{5,29},{6,30},{7,31},{8,0},{9,1... | collective-permute-start | bytes 1572872 | tf_op jit(solution)/shard_map/ppermute | solution.py:35
  36.6 4.4 %collective-permute-start.33 = (bf16[528,512]{1,0:T(8,128)(2,1)}, bf16[528,512]{1,0:T(8,128)(2,1)}, u32[]{:S(2)}, u32[]{:S(2)}) collective-permute-start(bf16[528,512]{1,0:T(8,128)(2,1)} %collective-permute-done.27.refs_2_), channel_id=1, source_target_pairs={{0,3},{1,0},{2,1},{3,2},{4,7},{5,4},{6,5},{7,6},{8,11},{9,8},{10,9... | collective-permute-start | bytes 1622024 | tf_op jit(solution)/shard_map/ppermute | solution.py:35
  41.0 7.1 %collective-permute-done.16.refs_1_ = bf16[256,1024]{1,0:T(8,128)(2,1)S(1)} collective-permute-done((bf16[256,1024]{1,0:T(8,128)(2,1)S(1)}, bf16[256,1024]{1,0:T(8,128)(2,1)S(1)}, u32[]{:S(2)}, u32[]{:S(2)}) %collective-permute-start.16) | collective-permute-done | bytes 524320 | tf_op jit(solution)/shard_map/ppermute | solution.py:35
  54.7 11.8 %collective-permute-done.14.refs_0_ = bf16[128,1024]{1,0:T(8,128)(2,1)S(1)} collective-permute-done((bf16[128,1024]{1,0:T(8,128)(2,1)S(1)}, bf16[128,1024]{1,0:T(8,128)(2,1)S(1)}, u32[]{:S(2)}, u32[]{:S(2)}) %collective-permute-start.14) | collective-permute-done | bytes 262176 | tf_op jit(solution)/shard_map/ppermute | solution.py:35
  66.5 4.3 %collective-permute-start.37 = (bf16[528,512]{1,0:T(8,128)(2,1)}, bf16[528,512]{1,0:T(8,128)(2,1)S(1)}, u32[]{:S(2)}, u32[]{:S(2)}) collective-permute-start(bf16[528,512]{1,0:T(8,128)(2,1)} %collective-permute-done.27.refs_2_), channel_id=1, source_target_pairs={{0,1},{1,2},{2,3},{3,0},{4,5},{5,6},{6,7},{7,4},{8,9},{9,10},{10,1... | collective-permute-start | bytes 1622024 | tf_op jit(solution)/shard_map/ppermute | solution.py:35
  79.5 3.4 %copy-done = bf16[8192,512]{1,0:T(8,128)(2,1)S(1)} copy-done((bf16[8192,512]{1,0:T(8,128)(2,1)S(1)}, bf16[8192,512]{1,0:T(8,128)(2,1)}, u32[]{:S(2)}) %copy-start) | copy-done | bytes 8388632
  83.9 5.4 %y_stage.3 = (f32[256,512]{1,0:T(8,128)S(1)}, f32[256,512]{1,0:T(8,128)S(1)}) custom-call(s32[5]{0:T(128)S(1)} %stack.96.where, bf16[256,1024]{1,0:T(8,128)(2,1)S(1)} %cut_rows.3.refs_0_, bf16[256,1024]{1,0:T(8,128)(2,1)S(1)} %copy-done.6, bf16[256,1024]{1,0:T(8,128)(2,1)S(1)} %collective-permute-done.13.refs_2_, ...), custom_call_target="tpu_custom_call" | custom-call | flops 2147483648 | bytes 10485760 | tf_op jit(solution)/shard_map/y_stage/pallas_call | solution.py:211
  89.3 4.3 %collective-permute-done.15.refs_0_ = bf16[128,1024]{1,0:T(8,128)(2,1)} collective-permute-done((bf16[128,1024]{1,0:T(8,128)(2,1)S(1)}, bf16[128,1024]{1,0:T(8,128)(2,1)}, u32[]{:S(2)}, u32[]{:S(2)}) %collective-permute-start.15) | collective-permute-done | bytes 262176 | tf_op jit(solution)/shard_map/ppermute | solution.py:35
  93.6 4.7 %y_stage.4 = (f32[256,512]{1,0:T(8,128)S(1)}, f32[256,512]{1,0:T(8,128)S(1)}) custom-call(s32[4]{0:T(128)S(1)} %pad_add_fusion.1.where, bf16[128,1024]{1,0:T(8,128)(2,1)S(1)} %collective-permute-done.14.refs_0_, bf16[128,1024]{1,0:T(8,128)(2,1)} %collective-permute-done.17.refs_1_, bf16[256,1024]{1,0:T(8,128)(2,1)} %collective-permute-done.21.refs_2_, ...), custom_call_target="tpu_custom_call" | custom-call | flops 1610612736 | bytes 8388608 | tf_op jit(solution)/shard_map/y_stage/pallas_call | solution.py:211
  98.9 3.4 %y_stage.5 = f32[256,256]{1,0:T(8,128)S(1)} custom-call(s32[2]{0:T(128)S(1)} %pad_add_fusion.where, bf16[128,1024]{1,0:T(8,128)(2,1)} %collective-permute-done.15.refs_0_, bf16[128,1024]{1,0:T(8,128)(2,1)S(1)} %collective-permute-done.18.refs_1_, bf16[8192,512]{1,0:T(8,128)(2,1)S(1)} %copy-done.1, bf16[8192,512]{1,0:T(8,128)(2,1)} %collective-permute-done.19.refs_5_.refs_3_, ...), custom_call_target="tpu_custom_call" | custom-call | flops 536870912 | bytes 4194304 | tf_op jit(solution)/shard_map/y_stage/pallas_call | solution.py:211
  104.1 3.7 %collective-permute-done.23 = bf16[256,256]{1,0:T(8,128)(2,1)S(1)} collective-permute-done((bf16[256,256]{1,0:T(8,128)(2,1)S(1)}, bf16[256,256]{1,0:T(8,128)(2,1)S(1)}, u32[]{:S(2)}, u32[]{:S(2)}) %collective-permute-start.23) | collective-permute-done | bytes 131104 | tf_op jit(solution)/shard_map/ppermute | solution.py:35
  109.1 5.0 %collective-permute-start.24 = (bf16[256,256]{1,0:T(8,128)(2,1)S(1)}, bf16[256,256]{1,0:T(8,128)(2,1)S(1)}, u32[]{:S(2)}, u32[]{:S(2)}) collective-permute-start(bf16[256,256]{1,0:T(8,128)(2,1)S(1)} %fusion), channel_id=1, source_target_pairs={{0,24},{1,25},{2,26},{3,27},{4,28},{5,29},{6,30},{7,31},{8,16},{9,... | collective-permute-start | bytes 393224 | tf_op jit(solution)/shard_map/ppermute | solution.py:35
  114.1 13.9 %collective-permute-done.24 = bf16[256,256]{1,0:T(8,128)(2,1)S(1)} collective-permute-done((bf16[256,256]{1,0:T(8,128)(2,1)S(1)}, bf16[256,256]{1,0:T(8,128)(2,1)S(1)}, u32[]{:S(2)}, u32[]{:S(2)}) %collective-permute-start.24) | collective-permute-done | bytes 131104 | tf_op jit(solution)/shard_map/ppermute | solution.py:35
  128.9 3.4 %collective-permute-start.25 = (bf16[256,256]{1,0:T(8,128)(2,1)S(1)}, bf16[256,256]{1,0:T(8,128)(2,1)S(1)}, u32[]{:S(2)}, u32[]{:S(2)}) collective-permute-start(bf16[256,256]{1,0:T(8,128)(2,1)S(1)} %fusion.1), channel_id=1, source_target_pairs={{0,32},{1,33},{2,34},{3,35},{4,36},{5,37},{6,38},{7,39},{8,40},{9,... | collective-permute-start | bytes 393224 | tf_op jit(solution)/shard_map/ppermute | solution.py:35
  135.3 3.4 %collective-permute-start.7 = (bf16[256,1024]{1,0:T(8,128)(2,1)S(1)}, bf16[256,1024]{1,0:T(8,128)(2,1)}, u32[]{:S(2)}, u32[]{:S(2)}) collective-permute-start(bf16[256,1024]{1,0:T(8,128)(2,1)S(1)} %collective-permute-done.2.refs_0_), channel_id=1, source_target_pairs={{0,32},{1,33},{2,34},{3,35},{4,36},{5,37},{6,38},{7,39},{8,40},{9,... | collective-permute-start | bytes 1572872 | tf_op jit(solution)/shard_map/ppermute | solution.py:35
  140.4 3.6 %collective-permute-start.26 = (bf16[256,256]{1,0:T(8,128)(2,1)S(1)}, bf16[256,256]{1,0:T(8,128)(2,1)S(1)}, u32[]{:S(2)}, u32[]{:S(2)}) collective-permute-start(bf16[256,256]{1,0:T(8,128)(2,1)S(1)} %add_convert_fusion), channel_id=1, source_target_pairs={{0,64},{1,65},{2,66},{3,67},{4,68},{5,69},{6,70},{7,71},{8,72},{9,... | collective-permute-start | bytes 393224 | tf_op jit(solution)/shard_map/ppermute | solution.py:35
  146.4 4.9 %collective-permute-done.26 = bf16[256,256]{1,0:T(8,128)(2,1)S(1)} collective-permute-done((bf16[256,256]{1,0:T(8,128)(2,1)S(1)}, bf16[256,256]{1,0:T(8,128)(2,1)S(1)}, u32[]{:S(2)}, u32[]{:S(2)}) %collective-permute-start.26) | collective-permute-done | bytes 131104 | tf_op jit(solution)/shard_map/ppermute | solution.py:35
  153.9 7.4 %collective-permute-start.29 = (bf16[2,256,256]{2,1,0:T(8,128)(2,1)S(1)}, bf16[2,256,256]{2,1,0:T(8,128)(2,1)}, u32[]{:S(2)}, u32[]{:S(2)}) collective-permute-start(bf16[2,256,256]{2,1,0:T(8,128)(2,1)S(1)} %pad_maximum_fusion.1.refs_0_), channel_id=1, source_target_pairs={{0,3},{1,0},{2,1},{3,2},{4,7},{5,4},{6,5},{7,6},{8,11},{9,8},{10,9... | collective-permute-start | bytes 786440 | tf_op jit(solution)/shard_map/ppermute | solution.py:35
  163.1 3.3 %collective-permute-start.8 = (bf16[256,1024]{1,0:T(8,128)(2,1)}, bf16[256,1024]{1,0:T(8,128)(2,1)S(1)}, u32[]{:S(2)}, u32[]{:S(2)}) collective-permute-start(bf16[256,1024]{1,0:T(8,128)(2,1)} %collective-permute-done.7.refs_3_), channel_id=1, source_target_pairs={{0,24},{1,25},{2,26},{3,27},{4,28},{5,29},{6,30},{7,31},{8,0},{9,1... | collective-permute-start | bytes 1572872 | tf_op jit(solution)/shard_map/ppermute | solution.py:35
  175.4 4.1 %z_stage.3.refs_5_.refs_7_ = bf16[6,256,1024]{2,1,0:T(8,128)(2,1)S(1)} custom-call(s32[1]{0:T(128)} %bitcast.core, bf16[2,256,256]{2,1,0:T(8,128)(2,1)} %collective-permute-done.29.refs_0_, bf16[2,256,256]{2,1,0:T(8,128)(2,1)} %collective-permute-done.30.refs_1_, bf16[2,256,256]{2,1,0:T(8,128)(2,1)} %collective-permute-done.31.refs_2_, ...), custom_call_target="tpu_custom_call" | custom-call | flops 1610612736 | bytes 12582912 | tf_op jit(solution)/shard_map/z_stage/pallas_call | solution.py:245
  179.6 4.3 %out_stage.3 = (f32[1024,512]{1,0:T(8,128)S(1)}, f32[1024,512]{1,0:T(8,128)S(1)}) custom-call(s32[5]{0:T(128)S(1)} %stack.104.core, bf16[256,1024]{1,0:T(8,128)(2,1)S(1)} %copy-done.26, bf16[256,1024]{1,0:T(8,128)(2,1)S(1)} %copy-done.24, bf16[256,1024]{1,0:T(8,128)(2,1)S(1)} %copy-done.22, bf16[256,1024]{1,0:T(8,128)(2,1)} %collective-permute-done.7.refs_3_, ...), custom_call_target="tpu_custom_call" | custom-call | flops 2147483648 | bytes 8388608 | tf_op jit(solution)/shard_map/out_stage/pallas_call | solution.py:310
  (150 shorter events, 63.6 us)
Async XLA Ops:
  0.0 76.4 %collective-permute-start.19 = (bf16[8192,512]{1,0:T(8,128)(2,1)}, bf16[8192,512]{1,0:T(8,128)(2,1)}, u32[]{:S(2)}, u32[]{:S(2)}) collective-permute-start(bf16[8192,512]{1,0:T(8,128)(2,1)} %refs_2_.1), channel_id=1, source_target_pairs={{0,4},{1,5},{2,6},{3,7},{4,0},{5,1},{6,2},{7,3},{8,12},{9,13},{10,... | collective-permute-start | bytes 25165832 | tf_op jit(solution)/shard_map/ppermute | solution.py:35
  17.0 18.9 %collective-permute-start.36 = (bf16[528,512]{1,0:T(8,128)(2,1)S(1)}, bf16[528,512]{1,0:T(8,128)(2,1)}, u32[]{:S(2)}, u32[]{:S(2)}) collective-permute-start(bf16[528,512]{1,0:T(8,128)(2,1)S(1)} %pad_maximum_fusion.refs_8_.refs_1_), channel_id=1, source_target_pairs={{0,1},{1,2},{2,3},{3,0},{4,5},{5,6},{6,7},{7,4},{8,9},{9,10},{10,1... | collective-permute-start | bytes 1622024 | tf_op jit(solution)/shard_map/ppermute | solution.py:35
  18.1 18.5 %collective-permute-start.20 = (bf16[256,1024]{1,0:T(8,128)(2,1)S(1)}, bf16[256,1024]{1,0:T(8,128)(2,1)}, u32[]{:S(2)}, u32[]{:S(2)}) collective-permute-start(bf16[256,1024]{1,0:T(8,128)(2,1)S(1)} %cut_rows.3.refs_0_), channel_id=1, source_target_pairs={{0,32},{1,33},{2,34},{3,35},{4,36},{5,37},{6,38},{7,39},{8,40},{9,... | collective-permute-start | bytes 1572872 | tf_op jit(solution)/shard_map/ppermute | solution.py:35
  21.4 19.6 %collective-permute-start.13 = (bf16[256,1024]{1,0:T(8,128)(2,1)S(1)}, bf16[256,1024]{1,0:T(8,128)(2,1)S(1)}, u32[]{:S(2)}, u32[]{:S(2)}) collective-permute-start(bf16[256,1024]{1,0:T(8,128)(2,1)S(1)} %cut_rows.3.refs_0_), channel_id=1, source_target_pairs={{0,8},{1,9},{2,10},{3,11},{4,12},{5,13},{6,14},{7,15},{8,16},{9,17... | collective-permute-start | bytes 1572872 | tf_op jit(solution)/shard_map/ppermute | solution.py:35
  40.9 30.4 %collective-permute-start.21 = (bf16[256,1024]{1,0:T(8,128)(2,1)}, bf16[256,1024]{1,0:T(8,128)(2,1)}, u32[]{:S(2)}, u32[]{:S(2)}) collective-permute-start(bf16[256,1024]{1,0:T(8,128)(2,1)} %collective-permute-done.20.refs_3_), channel_id=1, source_target_pairs={{0,24},{1,25},{2,26},{3,27},{4,28},{5,29},{6,30},{7,31},{8,0},{9,1... | collective-permute-start | bytes 1572872 | tf_op jit(solution)/shard_map/ppermute | solution.py:35
  48.1 26.6 %collective-permute-start.22 = (bf16[256,1024]{1,0:T(8,128)(2,1)}, bf16[256,1024]{1,0:T(8,128)(2,1)}, u32[]{:S(2)}, u32[]{:S(2)}) collective-permute-start(bf16[256,1024]{1,0:T(8,128)(2,1)} %collective-permute-done.20.refs_3_), channel_id=1, source_target_pairs={{0,8},{1,9},{2,10},{3,11},{4,12},{5,13},{6,14},{7,15},{8,16},{9,17... | collective-permute-start | bytes 1572872 | tf_op jit(solution)/shard_map/ppermute | solution.py:35
  48.5 18.0 %collective-permute-start.14 = (bf16[128,1024]{1,0:T(8,128)(2,1)S(1)}, bf16[128,1024]{1,0:T(8,128)(2,1)S(1)}, u32[]{:S(2)}, u32[]{:S(2)}) collective-permute-start(bf16[128,1024]{1,0:T(8,128)(2,1)S(1)} %slice.18), channel_id=1, source_target_pairs={{0,8},{1,9},{2,10},{3,11},{4,12},{5,13},{6,14},{7,15},{8,16},{9,17... | collective-permute-start | bytes 786440 | tf_op jit(solution)/shard_map/ppermute | solution.py:35
  52.4 18.5 %collective-permute-start.17 = (bf16[128,1024]{1,0:T(8,128)(2,1)}, bf16[128,1024]{1,0:T(8,128)(2,1)}, u32[]{:S(2)}, u32[]{:S(2)}) collective-permute-start(bf16[128,1024]{1,0:T(8,128)(2,1)} %slice.19), channel_id=1, source_target_pairs={{0,24},{1,25},{2,26},{3,27},{4,28},{5,29},{6,30},{7,31},{8,0},{9,1... | collective-permute-start | bytes 786440 | tf_op jit(solution)/shard_map/ppermute | solution.py:35
  66.5 35.8 %collective-permute-start.37 = (bf16[528,512]{1,0:T(8,128)(2,1)}, bf16[528,512]{1,0:T(8,128)(2,1)S(1)}, u32[]{:S(2)}, u32[]{:S(2)}) collective-permute-start(bf16[528,512]{1,0:T(8,128)(2,1)} %collective-permute-done.27.refs_2_), channel_id=1, source_target_pairs={{0,1},{1,2},{2,3},{3,0},{4,5},{5,6},{6,7},{7,4},{8,9},{9,10},{10,1... | collective-permute-start | bytes 1622024 | tf_op jit(solution)/shard_map/ppermute | solution.py:35
  70.9 32.7 %collective-permute-start.35 = (bf16[528,512]{1,0:T(8,128)(2,1)}, bf16[528,512]{1,0:T(8,128)(2,1)}, u32[]{:S(2)}, u32[]{:S(2)}) collective-permute-start(bf16[528,512]{1,0:T(8,128)(2,1)} %collective-permute-done.34.refs_5_), channel_id=1, source_target_pairs={{0,64},{1,65},{2,66},{3,67},{4,68},{5,69},{6,70},{7,71},{8,72},{9,... | collective-permute-start | bytes 1622024 | tf_op jit(solution)/shard_map/ppermute | solution.py:35
  71.3 22.2 %collective-permute-start.15 = (bf16[128,1024]{1,0:T(8,128)(2,1)S(1)}, bf16[128,1024]{1,0:T(8,128)(2,1)}, u32[]{:S(2)}, u32[]{:S(2)}) collective-permute-start(bf16[128,1024]{1,0:T(8,128)(2,1)S(1)} %collective-permute-done.14.refs_0_), channel_id=1, source_target_pairs={{0,32},{1,33},{2,34},{3,35},{4,36},{5,37},{6,38},{7,39},{8,40},{9,... | collective-permute-start | bytes 786440 | tf_op jit(solution)/shard_map/ppermute | solution.py:35
  74.7 28.9 %collective-permute-start.2 = (bf16[256,1024]{1,0:T(8,128)(2,1)}, bf16[256,1024]{1,0:T(8,128)(2,1)S(1)}, u32[]{:S(2)}, u32[]{:S(2)}) collective-permute-start(bf16[256,1024]{1,0:T(8,128)(2,1)} %copy-done.27), channel_id=1, source_target_pairs={{0,0},{1,3},{2,2},{3,1},{4,4},{5,7},{6,6},{7,5},{8,9},{9,8},{10,11... | collective-permute-start | bytes 1572872 | tf_op jit(solution)/shard_map/ppermute | solution.py:35
  76.4 21.9 %collective-permute-start.18 = (bf16[128,1024]{1,0:T(8,128)(2,1)}, bf16[128,1024]{1,0:T(8,128)(2,1)S(1)}, u32[]{:S(2)}, u32[]{:S(2)}) collective-permute-start(bf16[128,1024]{1,0:T(8,128)(2,1)} %collective-permute-done.17.refs_1_), channel_id=1, source_target_pairs={{0,32},{1,33},{2,34},{3,35},{4,36},{5,37},{6,38},{7,39},{8,40},{9,... | collective-permute-start | bytes 786440 | tf_op jit(solution)/shard_map/ppermute | solution.py:35
  103.6 28.6 %collective-permute-start.28 = (bf16[528,512]{1,0:T(8,128)(2,1)}, bf16[528,512]{1,0:T(8,128)(2,1)S(1)}, u32[]{:S(2)}, u32[]{:S(2)}) collective-permute-start(bf16[528,512]{1,0:T(8,128)(2,1)} %collective-permute-done.27.refs_2_), channel_id=1, source_target_pairs={{0,4},{1,5},{2,6},{3,7},{4,0},{5,1},{6,2},{7,3},{8,12},{9,13},{10,... | collective-permute-start | bytes 1622024 | tf_op jit(solution)/shard_map/ppermute | solution.py:35
  103.6 24.4 %collective-permute-start.42 = (bf16[528,512]{1,0:T(8,128)(2,1)}, bf16[528,512]{1,0:T(8,128)(2,1)S(1)}, u32[]{:S(2)}, u32[]{:S(2)}) collective-permute-start(bf16[528,512]{1,0:T(8,128)(2,1)} %collective-permute-done.36.refs_7_), channel_id=1, source_target_pairs={{0,4},{1,5},{2,6},{3,7},{4,0},{5,1},{6,2},{7,3},{8,12},{9,13},{10,... | collective-permute-start | bytes 1622024 | tf_op jit(solution)/shard_map/ppermute | solution.py:35
  107.9 24.4 %collective-permute-start.3 = (bf16[256,1024]{1,0:T(8,128)(2,1)S(1)}, bf16[256,1024]{1,0:T(8,128)(2,1)S(1)}, u32[]{:S(2)}, u32[]{:S(2)}) collective-permute-start(bf16[256,1024]{1,0:T(8,128)(2,1)S(1)} %collective-permute-done.2.refs_0_), channel_id=1, source_target_pairs={{0,8},{1,9},{2,10},{3,11},{4,12},{5,13},{6,14},{7,15},{8,16},{9,17... | collective-permute-start | bytes 1572872 | tf_op jit(solution)/shard_map/ppermute | solution.py:35
  109.1 18.9 %collective-permute-start.24 = (bf16[256,256]{1,0:T(8,128)(2,1)S(1)}, bf16[256,256]{1,0:T(8,128)(2,1)S(1)}, u32[]{:S(2)}, u32[]{:S(2)}) collective-permute-start(bf16[256,256]{1,0:T(8,128)(2,1)S(1)} %fusion), channel_id=1, source_target_pairs={{0,24},{1,25},{2,26},{3,27},{4,28},{5,29},{6,30},{7,31},{8,16},{9,... | collective-permute-start | bytes 393224 | tf_op jit(solution)/shard_map/ppermute | solution.py:35
  114.1 30.0 %collective-permute-start.39 = (bf16[528,512]{1,0:T(8,128)(2,1)}, bf16[528,512]{1,0:T(8,128)(2,1)S(1)}, u32[]{:S(2)}, u32[]{:S(2)}) collective-permute-start(bf16[528,512]{1,0:T(8,128)(2,1)} %collective-permute-done.33.refs_4_), channel_id=1, source_target_pairs={{0,4},{1,5},{2,6},{3,7},{4,0},{5,1},{6,2},{7,3},{8,12},{9,13},{10,... | collective-permute-start | bytes 1622024 | tf_op jit(solution)/shard_map/ppermute | solution.py:35
  132.2 20.8 %collective-permute-start.43 = (bf16[528,512]{1,0:T(8,128)(2,1)S(1)}, bf16[528,512]{1,0:T(8,128)(2,1)S(1)}, u32[]{:S(2)}, u32[]{:S(2)}) collective-permute-start(bf16[528,512]{1,0:T(8,128)(2,1)S(1)} %collective-permute-done.37.refs_8_), channel_id=1, source_target_pairs={{0,4},{1,5},{2,6},{3,7},{4,0},{5,1},{6,2},{7,3},{8,12},{9,13},{10,... | collective-permute-start | bytes 1622024 | tf_op jit(solution)/shard_map/ppermute | solution.py:35
  132.2 29.0 %collective-permute-start.41 = (bf16[528,512]{1,0:T(8,128)(2,1)}, bf16[528,512]{1,0:T(8,128)(2,1)S(1)}, u32[]{:S(2)}, u32[]{:S(2)}) collective-permute-start(bf16[528,512]{1,0:T(8,128)(2,1)} %collective-permute-done.35.refs_6_), channel_id=1, source_target_pairs={{0,4},{1,5},{2,6},{3,7},{4,0},{5,1},{6,2},{7,3},{8,12},{9,13},{10,... | collective-permute-start | bytes 1622024 | tf_op jit(solution)/shard_map/ppermute | solution.py:35
  135.3 26.7 %collective-permute-start.7 = (bf16[256,1024]{1,0:T(8,128)(2,1)S(1)}, bf16[256,1024]{1,0:T(8,128)(2,1)}, u32[]{:S(2)}, u32[]{:S(2)}) collective-permute-start(bf16[256,1024]{1,0:T(8,128)(2,1)S(1)} %collective-permute-done.2.refs_0_), channel_id=1, source_target_pairs={{0,32},{1,33},{2,34},{3,35},{4,36},{5,37},{6,38},{7,39},{8,40},{9,... | collective-permute-start | bytes 1572872 | tf_op jit(solution)/shard_map/ppermute | solution.py:35
  144.9 18.2 %collective-permute-start.6 = (bf16[128,1024]{1,0:T(8,128)(2,1)S(1)}, bf16[128,1024]{1,0:T(8,128)(2,1)S(1)}, u32[]{:S(2)}, u32[]{:S(2)}) collective-permute-start(bf16[128,1024]{1,0:T(8,128)(2,1)S(1)} %slice.17), channel_id=1, source_target_pairs={{0,24},{1,25},{2,26},{3,27},{4,28},{5,29},{6,30},{7,31},{8,0},{9,1... | collective-permute-start | bytes 786440 | tf_op jit(solution)/shard_map/ppermute | solution.py:35
  163.1 20.8 %collective-permute-start.11 = (bf16[256,1024]{1,0:T(8,128)(2,1)}, bf16[256,1024]{1,0:T(8,128)(2,1)S(1)}, u32[]{:S(2)}, u32[]{:S(2)}) collective-permute-start(bf16[256,1024]{1,0:T(8,128)(2,1)} %collective-permute-done.7.refs_3_), channel_id=1, source_target_pairs={{0,8},{1,9},{2,10},{3,11},{4,12},{5,13},{6,14},{7,15},{8,16},{9,17... | collective-permute-start | bytes 1572872 | tf_op jit(solution)/shard_map/ppermute | solution.py:35
  163.1 20.8 %collective-permute-start.8 = (bf16[256,1024]{1,0:T(8,128)(2,1)}, bf16[256,1024]{1,0:T(8,128)(2,1)S(1)}, u32[]{:S(2)}, u32[]{:S(2)}) collective-permute-start(bf16[256,1024]{1,0:T(8,128)(2,1)} %collective-permute-done.7.refs_3_), channel_id=1, source_target_pairs={{0,24},{1,25},{2,26},{3,27},{4,28},{5,29},{6,30},{7,31},{8,0},{9,1... | collective-permute-start | bytes 1572872 | tf_op jit(solution)/shard_map/ppermute | solution.py:35
  (49 other events, 596.6 us)
